TPU v7x, 128 devices: a whole 4x4x4 slice. The times are simulated.
128 devices in a mesh: grp: 8 (over x, core), seq: 16 (over y, z).
Axes of the slice: x: 4, y: 4, z: 4, core: 2. Of those that a mesh axis runs over, the one named last changes fastest.
Arguments:
- tokens: bfloat16 [32, 4, 5120], P(None, None, ('grp', 'seq')), may hold values from -90 to 90
- lengths: int32 [32], replicated, may hold values from 1 to 16384, as said below
- group_perm: int32 [32], replicated, may hold values from 0 to 31, as said below
- page_table: int32 [32, 128], replicated, may hold values from 0 to 31, as said below
- k_pool: bfloat16 [4096, 128, 1024], P(('grp', 'seq')), may hold values from -17 to 17
- v_pool: bfloat16 [4096, 128, 1024], P(('grp', 'seq')), may hold values from -7 to 7
- gain_in: float32 [5120], P(('grp', 'seq')), may hold values from 0.25 to 1.75
- qkv_weight: bfloat16 [5120, 7168], P('grp', 'seq'), may hold values from -0.15625 to 0.15625
- qkv_bias: float32 [7168], P('seq'), may hold values from -16 to 16
- o_weight: bfloat16 [5120, 5120], P('seq', 'grp'), may hold values from -0.078125 to 0.078125
- gain_mid: float32 [5120], P(('grp', 'seq')), may hold values from 0.25 to 1.75
- gate_weight: bfloat16 [5120, 13824], P('grp', 'seq'), may hold values from -0.078125 to 0.078125
- up_weight: bfloat16 [5120, 13824], P('grp', 'seq'), may hold values from -0.078125 to 0.078125
- down_weight: bfloat16 [13824, 5120], P('seq', 'grp'), may hold values from -0.0546875 to 0.0546875
Outputs:
- mixed: bfloat16 [32, 4, 5120], P(None, None, ('grp', 'seq'))
Inputs may be any that keep to these rules, and one draw needn't show every extreme that they name: `lengths`: one request holds exactly 16384 cached tokens. A permutation of the requests; request group_perm[i] belongs to group i // 4. `page_table`: page p of request r lies on the device with grp index g and seq index p // 8, where g is the group of r; the slots named for one device are all different.
All inputs are finite; a program needn't handle non-finite values.
Results may differ from a plain program's by a relative error of at most 0.015.
Values may be sent and summed in bfloat16 or wider, within the bound.
No kernel may reach another device: no remote copies, remote signals or barrier semaphores. Data moves between devices by JAX's collectives and lax.ppermute only.
A program may use at most 128 MiB of HBM per device.

v0:
```python
import jax
import jax.numpy as jnp
from jax import lax
from jax.sharding import PartitionSpec as P

D = 5120
HEADS = 40
KV_HEADS = 8
HEAD_DIM = 128
STEPS = 4
REQ_GRP = 4
SHARD_PAGES = 8
PAGE = 128
BLOCK_PAGES = 4
EPSILON = 1e-06
LOW_SCORE = -1e30
ROPE_BASE = 1000000.0


def rotary(values, position):
    half_dim = values.shape[-1] // 2
    exponent = jnp.arange(half_dim, dtype=jnp.float32) * (2.0 / values.shape[-1])
    inverse = jnp.exp(-exponent * jnp.log(jnp.float32(ROPE_BASE)))
    angle = position[..., None, None] * inverse
    cosine = jnp.cos(angle)
    sine_part = jnp.sin(angle)
    first_half = values[..., :half_dim]
    second_half = values[..., half_dim:]
    return jnp.concatenate(
        [
            first_half * cosine - second_half * sine_part,
            second_half * cosine + first_half * sine_part,
        ],
        axis=-1,
    )


def absorb(carried, query_mat, key_block, value_block, live_mask, score_scale):
    best_score, weight_sums, weighted = carried
    scores = (
        jnp.einsum("hqd,khd->hqk", query_mat, key_block, preferred_element_type=jnp.float32)
        * score_scale
    )
    scores = jnp.where(live_mask, scores, LOW_SCORE)
    fresh_top = jnp.maximum(best_score, jnp.max(scores, axis=-1))
    rescale = jnp.exp(best_score - fresh_top)
    weights = jnp.where(live_mask, jnp.exp(scores - fresh_top[..., None]), 0.0)
    weight_sums = weight_sums * rescale + jnp.sum(weights, axis=-1)
    weighted = weighted * rescale[..., None] + jnp.einsum(
        "hqk,khd->hqd",
        weights.astype(jnp.bfloat16),
        value_block,
        preferred_element_type=jnp.float32,
    )
    return (fresh_top, weight_sums, weighted)


def body(
    tokens,
    lengths,
    group_perm,
    page_table,
    k_pool,
    v_pool,
    gain_in,
    qkv_weight,
    qkv_bias,
    o_weight,
    gain_mid,
    gate_weight,
    up_weight,
    down_weight,
):
    n_seq = lax.axis_size("seq")
    grp_idx = lax.axis_index("grp")
    seq_idx = lax.axis_index("seq")
    group_q = HEADS // KV_HEADS
    query_rows = STEPS * group_q
    q_width = HEADS * HEAD_DIM
    kv_width = KV_HEADS * HEAD_DIM
    score_scale = HEAD_DIM ** (-0.5)
    sorted_rows = jnp.take(tokens, group_perm, axis=0).astype(jnp.float32)
    squares_in = lax.psum(jnp.sum(sorted_rows * sorted_rows, axis=-1), ("grp", "seq"))
    normed_in = (sorted_rows * lax.rsqrt(squares_in / D + EPSILON)[..., None] * gain_in).astype(
        jnp.bfloat16
    )
    proj_part = jnp.einsum(
        "rtc,ck->rtk",
        lax.all_gather(normed_in, "seq", axis=2, tiled=True),
        qkv_weight,
        preferred_element_type=jnp.float32,
    )
    proj_share = (
        lax.psum_scatter(
            proj_part.astype(jnp.bfloat16), "grp", scatter_dimension=0, tiled=True
        ).astype(jnp.float32)
        + qkv_bias
    )
    proj_full = lax.all_gather(proj_share, "seq", axis=2, tiled=True)
    members = lax.dynamic_slice_in_dim(group_perm, grp_idx * REQ_GRP, REQ_GRP)
    my_lengths = jnp.take(lengths, members)
    steps_range = jnp.arange(STEPS, dtype=jnp.int32)
    position = (my_lengths[:, None] + steps_range[None, :]).astype(jnp.float32)
    queries = rotary(
        proj_full[..., :q_width].reshape(REQ_GRP, STEPS, HEADS, HEAD_DIM), position
    ).astype(jnp.bfloat16)
    new_keys = rotary(
        proj_full[..., q_width : q_width + kv_width].reshape(REQ_GRP, STEPS, KV_HEADS, HEAD_DIM),
        position,
    ).astype(jnp.bfloat16)
    new_values = (
        proj_full[..., q_width + kv_width :]
        .reshape(REQ_GRP, STEPS, KV_HEADS, HEAD_DIM)
        .astype(jnp.bfloat16)
    )
    shard_rows = SHARD_PAGES * PAGE
    block_rows = BLOCK_PAGES * PAGE
    shard_base = seq_idx * shard_rows
    slot_table = lax.dynamic_slice_in_dim(
        jnp.take(page_table, members, axis=0), seq_idx * SHARD_PAGES, SHARD_PAGES, 1
    )
    is_last = seq_idx == n_seq - 1
    causal = (
        steps_range[None, :] <= (jnp.arange(query_rows, dtype=jnp.int32) // group_q)[:, None]
    ) & is_last
    causal = causal[None]
    query_all = (
        queries.reshape(REQ_GRP, STEPS, KV_HEADS, group_q, HEAD_DIM)
        .transpose(0, 2, 1, 3, 4)
        .reshape(REQ_GRP, KV_HEADS, query_rows, HEAD_DIM)
    )
    live_all = jnp.clip(my_lengths - shard_base, 0, shard_rows)
    block_offsets = jnp.arange(block_rows, dtype=jnp.int32)
    best_list = []
    sums_list = []
    acc_list = []
    for member in range(REQ_GRP):
        query_mat = query_all[member]
        length = my_lengths[member]
        member_slots = slot_table[member]
        initial = (
            jnp.full((KV_HEADS, query_rows), LOW_SCORE, jnp.float32),
            jnp.zeros((KV_HEADS, query_rows), jnp.float32),
            jnp.zeros((KV_HEADS, query_rows, HEAD_DIM), jnp.float32),
        )
        carried = absorb(
            initial, query_mat, new_keys[member], new_values[member], causal, score_scale
        )
        block_count = (live_all[member] + block_rows - 1) // block_rows

        def advance(
            block_index, running, member_slots=member_slots, length=length, query_mat=query_mat
        ):
            slot_ids = lax.dynamic_slice_in_dim(
                member_slots, block_index * BLOCK_PAGES, BLOCK_PAGES
            )
            key_block = jnp.take(k_pool, slot_ids, axis=0).reshape(block_rows, KV_HEADS, HEAD_DIM)
            value_block = jnp.take(v_pool, slot_ids, axis=0).reshape(block_rows, KV_HEADS, HEAD_DIM)
            positions = shard_base + block_index * block_rows + block_offsets
            return absorb(
                running,
                query_mat,
                key_block,
                value_block,
                (positions < length)[None, None, :],
                score_scale,
            )

        carried = lax.fori_loop(0, block_count, advance, carried)
        best_list.append(carried[0])
        sums_list.append(carried[1])
        acc_list.append(carried[2])
    best_score = jnp.stack(best_list)
    weight_sums = jnp.stack(sums_list)
    weighted = jnp.stack(acc_list)
    top_score = lax.pmax(best_score, "seq")
    factor = jnp.exp(best_score - top_score)
    weight_sums, weighted = (
        lax.psum((weight_sums * factor).astype(jnp.bfloat16), "seq").astype(jnp.float32),
        lax.psum((weighted * factor[..., None]).astype(jnp.bfloat16), "seq").astype(jnp.float32),
    )
    attended = (weighted / weight_sums[..., None]).reshape(
        REQ_GRP, KV_HEADS, STEPS, group_q, HEAD_DIM
    )
    attended = (
        attended.transpose(0, 2, 1, 3, 4).reshape(REQ_GRP, STEPS, q_width).astype(jnp.bfloat16)
    )
    out_width = o_weight.shape[0]
    attended_cols = lax.dynamic_slice_in_dim(attended, seq_idx * out_width, out_width, 2)
    out_terms = jnp.einsum(
        "rtc,cd->rtd",
        lax.all_gather(attended_cols, "grp", axis=0, tiled=True),
        o_weight,
        preferred_element_type=jnp.float32,
    )
    attn_sum = lax.psum_scatter(
        out_terms.astype(jnp.bfloat16), "seq", scatter_dimension=2, tiled=True
    ).astype(jnp.float32)
    residual = sorted_rows + attn_sum
    squares_mid = lax.psum(jnp.sum(residual * residual, axis=-1), ("grp", "seq"))
    normed_mid = (residual * lax.rsqrt(squares_mid / D + EPSILON)[..., None] * gain_mid).astype(
        jnp.bfloat16
    )
    segment = lax.all_gather(normed_mid, "seq", axis=2, tiled=True)
    gate_part = jnp.einsum("rtc,cf->rtf", segment, gate_weight, preferred_element_type=jnp.float32)
    up_part = jnp.einsum("rtc,cf->rtf", segment, up_weight, preferred_element_type=jnp.float32)
    gate_sum, up_sum = (
        lax.psum(gate_part.astype(jnp.bfloat16), "grp").astype(jnp.float32),
        lax.psum(up_part.astype(jnp.bfloat16), "grp").astype(jnp.float32),
    )
    hidden = (jax.nn.silu(gate_sum) * up_sum).astype(jnp.bfloat16)
    down_terms = jnp.einsum("rtf,fd->rtd", hidden, down_weight, preferred_element_type=jnp.float32)
    down_sum = lax.psum_scatter(
        down_terms.astype(jnp.bfloat16), "seq", scatter_dimension=2, tiled=True
    ).astype(jnp.float32)
    restore = jnp.argsort(group_perm)
    return jnp.take(residual + down_sum, restore, axis=0).astype(jnp.bfloat16)


def solution(mesh):
    return jax.shard_map(
        body,
        mesh=mesh,
        in_specs=(
            P(None, None, ("grp", "seq")),
            P(),
            P(),
            P(),
            P(("grp", "seq"), None, None),
            P(("grp", "seq"), None, None),
            P(("grp", "seq")),
            P("grp", "seq"),
            P("seq"),
            P("seq", "grp"),
            P(("grp", "seq")),
            P("grp", "seq"),
            P("grp", "seq"),
            P("seq", "grp"),
        ),
        out_specs=P(None, None, ("grp", "seq")),
        check_vma=False,
    )
```

profile of v0, /device:TPU:0, one launch (start us, length us, event | category | flops | bytes accessed | tf_op | source)
XLA Modules:
  0.0 875.4 jit_solution(11767665669221930165)
XLA Ops:
  9.5 68.2 %psum.42 = f32[32,4]{0,1:T(4,128)S(1)} all-reduce(f32[32,4]{0,1:T(4,128)S(1)} %fusion.75), channel_id=1, replica_groups=mesh['grp'=8,'seq'=16] {'grp','seq'}, use_global_device_ids=true, to_apply=%region_2.3 | all-reduce | flops 128 | bytes 1024 | tf_op jit(solution)/shard_map/psum | solution.py:83
  78.6 21.7 %all_gather.12 = bf16[32,4,640]{0,1,2:T(4,128)(2,1)S(1)} all-gather(bf16[32,4,40]{0,1,2:T(4,128)(2,1)S(1)} %copy.177), channel_id=1, replica_groups=mesh['grp'=8,'seq'=16] {'seq'}, dimensions={2}, use_global_device_ids=true | all-gather | bytes 174080 | tf_op jit(solution)/shard_map/all_gather | solution.py:89
  112.0 48.4 %all-reduce.12.cloned.1.call-done = bf16[32,4,448]{2,0,1:T(8,128)(2,1)} async-done(((bf16[32,4,448]{2,0,1:T(8,128)(2,1)}), bf16[32,4,448]{2,0,1:T(8,128)(2,1)}) %all-reduce.12.cloned.1.call-update) | async-done | bytes 114704
  161.7 80.0 %all_gather.13 = f32[4,4,7168]{1,0,2:T(4,128)S(1)} all-gather(f32[4,4,448]{1,0,2:T(4,128)S(1)} %copy.179), channel_id=1, replica_groups=mesh['grp'=8,'seq'=16] {'seq'}, dimensions={2}, use_global_device_ids=true | all-gather | bytes 487424 | tf_op jit(solution)/shard_map/all_gather | solution.py:99
  241.8 4.1 convert.21
  245.8 4.5 slice.158
  251.3 9.4 %fusion.141 = (f32[4,4,40,64]{1,0,3,2:T(4,128)}, f32[4,4,40,64]{1,0,3,2:T(4,128)}) fusion(f32[4,4,40,128]{1,0,3,2:T(4,128)} %bitcast.196), kind=kLoop, calls=%fused_computation.266 | loop fusion | bytes 655360 | tf_op jit(solution)/shard_map/slice | solution.py:28
  260.7 4.1 copy.227
  264.8 4.1 copy.226
  271.7 4.4 fusion.142
  280.1 22.0 %while.63 = (s32[]{:T(128)}, f32[8,20]{1,0:T(8,128)S(1)}, f32[8,20]{1,0:T(8,128)S(1)}, f32[8,20,128]{2,1,0:T(8,128)S(1)}, s32[]{:T(128)}, /*index=5*/s32[]{:T(12...) while((s32[]{:T(128)}, f32[8,20]{1,0:T(8,128)S(1)}, ...), condition=%wide.region_27.29_spmd.clone, body=%wide.region_24.28_spmd.clone.sunk | while | flops 43772256 | bytes 15884615 | solution.py:169
  280.9 4.0 gather_fusion.7
  303.7 11.1 %while.61 = (s32[]{:T(128)}, f32[8,20]{1,0:T(8,128)S(1)}, f32[8,20]{1,0:T(8,128)S(1)}, f32[8,20,128]{2,1,0:T(8,128)S(1)}, s32[]{:T(128)}, /*index=5*/s32[]{:T(12...) while((s32[]{:T(128)}, f32[8,20]{1,0:T(8,128)S(1)}, ...), condition=%wide.region_15.17_spmd.clone, body=%wide.region_12.16_spmd.clone.sunk | while | flops 43772256 | bytes 15884615 | solution.py:169
  315.8 12.8 %while.62 = (s32[]{:T(128)}, f32[8,20]{1,0:T(8,128)S(1)}, f32[8,20]{1,0:T(8,128)S(1)}, f32[8,20,128]{2,1,0:T(8,128)S(1)}, s32[]{:T(128)}, /*index=5*/s32[]{:T(12...) while((s32[]{:T(128)}, f32[8,20]{1,0:T(8,128)S(1)}, ...), condition=%wide.region_21.23_spmd.clone, body=%wide.region_18.22_spmd.clone.sunk | while | flops 43772256 | bytes 16048483 | solution.py:169
  330.3 23.8 %while.60 = (s32[]{:T(128)}, f32[8,20]{1,0:T(8,128)S(1)}, f32[8,20]{1,0:T(8,128)S(1)}, f32[8,20,128]{2,1,0:T(8,128)S(1)}, s32[]{:T(128)}, /*index=5*/s32[]{:T(12...) while((s32[]{:T(128)}, f32[8,20]{1,0:T(8,128)S(1)}, ...), condition=%wide.region_9.11_spmd.clone, body=%wide.region_6.10_spmd.clone.sunk | while | flops 43772256 | bytes 16048483 | solution.py:169
  354.1 69.7 %pmax.7 = f32[4,8,20]{2,1,0:T(8,128)S(1)} all-reduce(f32[4,8,20]{2,1,0:T(8,128)S(1)} %pad_maximum_fusion), channel_id=1, replica_groups=mesh['grp'=8,'seq'=16] {'seq'}, use_global_device_ids=true, to_apply=%region_28.30 | all-reduce | flops 640 | bytes 5120 | tf_op jit(solution)/shard_map/pmax | solution.py:176
  425.7 36.1 %psum.44 = bf16[4,8,20]{2,1,0:T(8,128)(2,1)S(1)} all-reduce(bf16[4,8,20]{2,1,0:T(8,128)(2,1)S(1)} %get-tuple-element.666), channel_id=1, replica_groups=mesh['grp'=8,'seq'=16] {'seq'}, use_global_device_ids=true, to_apply=%region_30.32 | all-reduce | flops 640 | bytes 2560 | tf_op jit(solution)/shard_map/psum | solution.py:179
  461.9 70.2 %all-reduce.10.cloned.1.call-done = bf16[4,8,20,128]{3,1,2,0:T(8,128)(2,1)} async-done(((bf16[4,8,20,128]{3,1,2,0:T(8,128)(2,1)}), bf16[4,8,20,128]{3,1,2,0:T(8,128)(2,1)}) %all-reduce.10.cloned.1.call-update) | async-done | bytes 163856 | tf_op jit(solution)/shard_map/psum | solution.py:180
  533.4 13.0 %all_gather.14 = bf16[32,4,320]{2,1,0:T(4,128)(2,1)S(1)} all-gather(bf16[4,4,320]{2,1,0:T(4,128)(2,1)S(1)} %constant_dynamic-slice_fusion), channel_id=1, replica_groups=mesh['grp'=8,'seq'=16] {'grp'}, dimensions={0}, use_global_device_ids=true | all-gather | bytes 92160 | tf_op jit(solution)/shard_map/all_gather | solution.py:192
  552.0 78.8 %all-reduce.14.cloned.1.call-done = bf16[32,4,640]{2,0,1:T(8,128)(2,1)} async-done(((bf16[32,4,640]{2,0,1:T(8,128)(2,1)}), bf16[32,4,640]{2,0,1:T(8,128)(2,1)}) %all-reduce.14.cloned.1.call-update) | async-done | bytes 163856
  631.8 62.7 %psum.45 = f32[32,4]{0,1:T(4,128)S(1)} all-reduce(f32[32,4]{0,1:T(4,128)S(1)} %multiply_reduce_fusion), channel_id=1, replica_groups=mesh['grp'=8,'seq'=16] {'grp','seq'}, use_global_device_ids=true, to_apply=%region_33.35 | all-reduce | flops 128 | bytes 1024 | tf_op jit(solution)/shard_map/psum | solution.py:200
  695.6 23.7 %all_gather.15 = bf16[32,4,640]{0,1,2:T(4,128)(2,1)S(1)} all-gather(bf16[32,4,40]{0,1,2:T(4,128)(2,1)S(1)} %copy.213), channel_id=1, replica_groups=mesh['grp'=8,'seq'=16] {'seq'}, dimensions={2}, use_global_device_ids=true | all-gather | bytes 174080 | tf_op jit(solution)/shard_map/all_gather | solution.py:204
  722.1 58.0 %all-reduce.18.cloned.1.call-done = (bf16[32,4,864]{2,0,1:T(8,128)(2,1)}, bf16[32,4,864]{2,0,1:T(8,128)(2,1)}) async-done(((bf16[32,4,864]{2,0,1:T(8,128)(2,1)}, bf16[32,4,864]{2,0,1:T(8,128)(2,1)}), (bf16[32,4,864]{2,0,1:T(8,128)(2,1)}, bf16[32,4,864]{2,0,1:T(8,128)(2,1)})) %all-reduce.18.cloned.1.call-update) | async-done | bytes 442384 | tf_op jit(solution)/shard_map/psum | solution.py:209
  782.6 84.0 %all-reduce.16.cloned.1.call-done = bf16[32,4,640]{2,0,1:T(8,128)(2,1)} async-done(((bf16[32,4,640]{2,0,1:T(8,128)(2,1)}), bf16[32,4,640]{2,0,1:T(8,128)(2,1)}) %all-reduce.16.cloned.1.call-update) | async-done | bytes 163856
  (212 shorter events, 108.1 us)
Async XLA Ops:
  6.5 713.1 %copy-start = (bf16[640,864]{0,1:T(8,128)(2,1)S(1)}, bf16[640,864]{0,1:T(8,128)(2,1)}, u32[]{:S(2)}) copy-start(bf16[640,864]{0,1:T(8,128)(2,1)} %param.36) | copy-start | bytes 3317764
  6.5 154.0 %all-reduce.12.cloned.1.call-start = ((), (), s32[]{:S(2)}) async-start(), calls=%async_computation.1 | async-start | bytes 262144
  7.3 70.4 %copy-start.8 = (pred[32]{0:T(512)(128)(4,1)}, pred[32]{0:T(512)(128)(4,1)S(1)}, u32[]{:S(2)}) copy-start(pred[32]{0:T(512)(128)(4,1)S(1)} %compare_and_fusion.5) | copy-start | bytes 100
  102.5 429.5 %all-reduce.10.cloned.1.call-start = ((), (), s32[]{:S(2)}) async-start(), calls=%async_computation | async-start | bytes 327680 | tf_op jit(solution)/shard_map/psum | solution.py:180
  106.8 208.1 %copy-start.5 = (pred[20,4]{0,1:T(4,128)(4,1)}, pred[20,4]{0,1:T(4,128)(4,1)S(1)}, u32[]{:S(2)}) copy-start(pred[20,4]{0,1:T(4,128)(4,1)S(1)} %fusion.119) | copy-start | bytes 244
  270.4 9.5 %copy-start.2 = (f32[8,20,4]{1,2,0:T(4,128)}, f32[8,20,4]{1,2,0:T(4,128)S(1)}, u32[]{:S(2)}) copy-start(f32[8,20,4]{1,2,0:T(4,128)S(1)} %get-tuple-element.733) | copy-start | bytes 7684
  270.8 7.8 copy-start.6
  271.1 7.5 copy-start.7
  325.8 1.2 copy-start.4
  330.2 219.4 %copy-start.11 = (s32[32]{0:T(128)S(1)}, s32[32]{0:T(128)}, u32[]{:S(2)}) copy-start(s32[32]{0:T(128)} %param.26) | copy-start | bytes 388
  330.3 300.5 %copy-start.9 = (pred[32]{0:T(512)(128)(4,1)S(1)}, pred[32]{0:T(512)(128)(4,1)}, u32[]{:S(2)}) copy-start(pred[32]{0:T(512)(128)(4,1)} %copy-done.8) | copy-start | bytes 100
  330.3 364.3 %copy-start.10 = (f32[40]{0:T(128)S(1)}, f32[40]{0:T(128)}, u32[]{:S(2)}) copy-start(f32[40]{0:T(128)} %param.34) | copy-start | bytes 484
  339.7 0.8 copy-start.3
  351.6 0.8 copy-start.3
  354.1 366.7 %copy-start.1 = (bf16[640,864]{0,1:T(8,128)(2,1)S(1)}, bf16[640,864]{0,1:T(8,128)(2,1)}, u32[]{:S(2)}) copy-start(bf16[640,864]{0,1:T(8,128)(2,1)} %param.35) | copy-start | bytes 3317764
  425.6 205.1 %all-reduce.14.cloned.1.call-start = ((), (), s32[]{:S(2)}) async-start(), calls=%async_computation.2 | async-start | bytes 327680
  548.3 231.7 %all-reduce.18.cloned.1.call-start = ((), (), s32[]{:S(2)}) async-start(), calls=%async_computation.4 | async-start | bytes 917504 | tf_op jit(solution)/shard_map/psum | solution.py:209
  722.0 144.6 %all-reduce.16.cloned.1.call-start = ((), (), s32[]{:S(2)}) async-start(), calls=%async_computation.3 | async-start | bytes 327680
Sparse Core Ops, SparseCore 0:
  102.6 57.7 all-reduce.11
  425.8 106.2 all-reduce.9
  548.5 82.2 all-reduce.13
  722.1 57.8 all-reduce.17
  783.1 83.4 all-reduce.15
where the time goes:
time: 878 us; the launch traced here: 875 us
  blocking collectives  375 us (43%)
  waiting for transfers between devices  339 us (39%)
  local copies, waits for them, and re-layouts  93.7 us (11%)
  other arithmetic  29.9 us (3%)
  matrix products  18.9 us (2%)
  between operations  17.5 us (2%)
    unnamed x8, waiting for transfers between devices  211 us
    all_gather x1, blocking collectives, body(): proj_full = lax.all_gather(proj_share, 'seq', axis=2, tiled=True)  80 us
    psum x1, waiting for transfers between devices, body(): lax.psum((weighted * factor[..., None]).astype(jnp.bfloat16), 'seq')  70.2 us
    pmax x1, blocking collectives, body(): top_score = lax.pmax(best_score, 'seq')  69.7 us
    psum x1, blocking collectives, body(): lax.psum(jnp.sum(sorted_rows * sorted_rows, axis=-1), ('grp', 'seq'))  68.2 us
    psum x1, blocking collectives, body(): lax.psum(jnp.sum(residual * residual, axis=-1), ('grp', 'seq'))  62.7 us
    psum x1, waiting for transfers between devices, body(): lax.psum(up_part.astype(jnp.bfloat16), 'grp').astype(jnp.float32)  58 us
    psum x1, blocking collectives, body(): lax.psum((weight_sums * factor).astype(jnp.bfloat16), 'seq')  36.1 us
  transfers between devices with their start and end apart: 5, of which 5 were waited for; matrix products, arithmetic and copies ran while one was open for 1% of the time, Pallas kernels for 0%

commit v1 on v0

--- a/solution.py
+++ b/solution.py
@@ -96,7 +96,9 @@
         ).astype(jnp.float32)
         + qkv_bias
     )
-    proj_full = lax.all_gather(proj_share, "seq", axis=2, tiled=True)
+    proj_full = jnp.concatenate(
+        lax.all_to_all(jnp.stack([proj_share] * lax.axis_size("seq")), "seq", 0, 0), axis=2
+    )
     members = lax.dynamic_slice_in_dim(group_perm, grp_idx * REQ_GRP, REQ_GRP)
     my_lengths = jnp.take(lengths, members)
     steps_range = jnp.arange(STEPS, dtype=jnp.int32)

time: 878 us -> 787 us (0.90)
  blocking collectives: 375 us -> 295 us
  local copies, waits for them, and re-layouts: 93.7 us -> 63.8 us
  waiting for transfers between devices: 339 us -> 352 us
    all_gather x1 -> x0, blocking collectives: 80 us -> none  [body(): proj_full = lax.all_gather(proj_share, 'seq', axis=2, tiled=True)]
    slice x9 -> x0, local copies, waits for them, and re-layouts: 21 us -> none  [the longest x2 9.53 us: rotary(): second_half = values[..., half_dim:]]
    unnamed x26 -> x38, local copies, waits for them, and re-layouts: 11.6 us -> 1.26 us
    all_to_all x0 -> x1, waiting for transfers between devices: none -> 9.88 us  [body(): lax.all_to_all(jnp.stack([proj_share] * lax.axis_size('seq')), 'seq', 0, 0)]
  transfers between devices with their start and end apart: 5 -> 6, of which waited for: 5 -> 6; matrix products, arithmetic and copies ran while one was open for 1% -> 1% of each run, Pallas kernels for 0% -> 0%
where the time goes in v1:
time: 787 us; the launch traced here: 785 us
  waiting for transfers between devices  352 us (45%)
  blocking collectives  295 us (37%)
  local copies, waits for them, and re-layouts  63.8 us (8%)
  other arithmetic  29.3 us (4%)
  matrix products  18.6 us (2%)
  between operations  17.6 us (2%)
    unnamed x8, waiting for transfers between devices  215 us
    psum x1, waiting for transfers between devices, body(): lax.psum((weighted * factor[..., None]).astype(jnp.bfloat16), 'seq')  69.7 us
    pmax x1, blocking collectives, body(): top_score = lax.pmax(best_score, 'seq')  69.5 us
    psum x1, blocking collectives, body(): lax.psum(jnp.sum(sorted_rows * sorted_rows, axis=-1), ('grp', 'seq'))  68.2 us
    psum x1, blocking collectives, body(): lax.psum(jnp.sum(residual * residual, axis=-1), ('grp', 'seq'))  62.7 us
    psum x1, waiting for transfers between devices, body(): lax.psum(up_part.astype(jnp.bfloat16), 'grp').astype(jnp.float32)  58 us
    psum x1, blocking collectives, body(): lax.psum((weight_sums * factor).astype(jnp.bfloat16), 'seq')  36.1 us
    gather x6, local copies, waits for them, and re-layouts, advance(): jnp.take(v_pool, slot_ids, axis=0).reshape(block_rows, KV_HEADS, HEAD_DIM)  24 us
  transfers between devices with their start and end apart: 6, of which 6 were waited for; matrix products, arithmetic and copies ran while one was open for 1% of the time, Pallas kernels for 0%

profile of v1, /device:TPU:0, one launch (start us, length us, event | category | flops | bytes accessed | tf_op | source)
XLA Modules:
  0.0 784.7 jit_solution(15766375314973922299)
XLA Ops:
  9.5 68.2 %psum.42 = f32[32,4]{0,1:T(4,128)S(1)} all-reduce(f32[32,4]{0,1:T(4,128)S(1)} %fusion.75), channel_id=1, replica_groups=mesh['grp'=8,'seq'=16] {'grp','seq'}, use_global_device_ids=true, to_apply=%region_2.3 | all-reduce | flops 128 | bytes 1024 | tf_op jit(solution)/shard_map/psum | solution.py:83
  78.6 21.7 %all_gather.9 = bf16[32,4,640]{0,1,2:T(4,128)(2,1)S(1)} all-gather(bf16[32,4,40]{0,1,2:T(4,128)(2,1)S(1)} %copy.107), channel_id=1, replica_groups=mesh['grp'=8,'seq'=16] {'seq'}, dimensions={2}, use_global_device_ids=true | all-gather | bytes 174080 | tf_op jit(solution)/shard_map/all_gather | solution.py:89
  109.3 51.3 %all-reduce.12.cloned.1.call-done = bf16[32,4,448]{2,0,1:T(8,128)(2,1)} async-done(((bf16[32,4,448]{2,0,1:T(8,128)(2,1)}), bf16[32,4,448]{2,0,1:T(8,128)(2,1)}) %all-reduce.12.cloned.1.call-update) | async-done | bytes 114704
  162.3 7.0 all-to-all-start
  169.5 9.9 %all-to-all-done = f32[16,4,4,448]{3,2,1,0:T(4,128)S(1)} async-done(((f32[16,4,4,448]{3,2,1,0:T(4,128)}), f32[16,4,4,448]{3,2,1,0:T(4,128)S(1)}, u32[]{:S(2)}, u32[]{:S(2)}) %all-to-all-start) | async-done | bytes 458784 | tf_op jit(solution)/shard_map/all_to_all | solution.py:100
  184.6 24.4 %while.63 = (s32[]{:T(128)}, f32[8,20]{1,0:T(8,128)S(1)}, f32[8,20]{1,0:T(8,128)S(1)}, f32[8,20,128]{2,1,0:T(8,128)S(1)}, s32[]{:T(128)}, /*index=5*/s32[]{:T(12...) while((s32[]{:T(128)}, f32[8,20]{1,0:T(8,128)S(1)}, ...), condition=%wide.region_27.29_spmd.clone, body=%wide.region_24.28_spmd.clone.sunk | while | flops 43772256 | bytes 20078948 | solution.py:171
  184.7 4.0 gather_fusion.6
  188.8 4.0 gather_fusion.7
  196.9 4.0 gather_fusion.6
  200.9 4.0 gather_fusion.7
  209.9 12.4 %while.62 = (s32[]{:T(128)}, f32[8,20]{1,0:T(8,128)S(1)}, f32[8,20]{1,0:T(8,128)S(1)}, f32[8,20,128]{2,1,0:T(8,128)S(1)}, s32[]{:T(128)}, /*index=5*/s32[]{:T(12...) while((s32[]{:T(128)}, f32[8,20]{1,0:T(8,128)S(1)}, ...), condition=%wide.region_21.23_spmd.clone, body=%wide.region_18.22_spmd.clone.sunk | while | flops 43772256 | bytes 20243128 | solution.py:171
  210.1 4.0 gather_fusion.4
  214.1 4.0 gather_fusion.5
  224.6 12.8 %while.61 = (s32[]{:T(128)}, f32[8,20]{1,0:T(8,128)S(1)}, f32[8,20]{1,0:T(8,128)S(1)}, f32[8,20,128]{2,1,0:T(8,128)S(1)}, s32[]{:T(128)}, /*index=5*/s32[]{:T(12...) while((s32[]{:T(128)}, f32[8,20]{1,0:T(8,128)S(1)}, ...), condition=%wide.region_15.17_spmd.clone, body=%wide.region_12.16_spmd.clone.sunk | while | flops 43772256 | bytes 20242816 | solution.py:171
  239.0 25.8 %while.60 = (s32[]{:T(128)}, f32[8,20]{1,0:T(8,128)S(1)}, f32[8,20]{1,0:T(8,128)S(1)}, f32[8,20,128]{2,1,0:T(8,128)S(1)}, s32[]{:T(128)}, /*index=5*/s32[]{:T(12...) while((s32[]{:T(128)}, f32[8,20]{1,0:T(8,128)S(1)}, ...), condition=%wide.region_9.11_spmd.clone, body=%wide.region_6.10_spmd.clone.sunk | while | flops 43772256 | bytes 20242816 | solution.py:171
  264.9 69.5 %pmax.7 = f32[4,8,20]{2,1,0:T(8,128)S(1)} all-reduce(f32[4,8,20]{2,1,0:T(8,128)S(1)} %pad_maximum_fusion), channel_id=1, replica_groups=mesh['grp'=8,'seq'=16] {'seq'}, use_global_device_ids=true, to_apply=%region_28.30 | all-reduce | flops 640 | bytes 5120 | tf_op jit(solution)/shard_map/pmax | solution.py:178
  336.3 36.1 %psum.44 = bf16[4,8,20]{2,1,0:T(8,128)(2,1)S(1)} all-reduce(bf16[4,8,20]{2,1,0:T(8,128)(2,1)S(1)} %get-tuple-element.622), channel_id=1, replica_groups=mesh['grp'=8,'seq'=16] {'seq'}, use_global_device_ids=true, to_apply=%region_30.32 | all-reduce | flops 640 | bytes 2560 | tf_op jit(solution)/shard_map/psum | solution.py:181
  372.6 69.7 %all-reduce.10.cloned.1.call-done = bf16[4,8,20,128]{3,1,2,0:T(8,128)(2,1)} async-done(((bf16[4,8,20,128]{3,1,2,0:T(8,128)(2,1)}), bf16[4,8,20,128]{3,1,2,0:T(8,128)(2,1)}) %all-reduce.10.cloned.1.call-update) | async-done | bytes 163856 | tf_op jit(solution)/shard_map/psum | solution.py:182
  443.6 13.0 %all_gather.10 = bf16[32,4,320]{2,1,0:T(4,128)(2,1)S(1)} all-gather(bf16[4,4,320]{2,1,0:T(4,128)(2,1)S(1)} %constant_dynamic-slice_fusion), channel_id=1, replica_groups=mesh['grp'=8,'seq'=16] {'grp'}, dimensions={0}, use_global_device_ids=true | all-gather | bytes 92160 | tf_op jit(solution)/shard_map/all_gather | solution.py:194
  460.5 79.5 %all-reduce.14.cloned.1.call-done = bf16[32,4,640]{2,0,1:T(8,128)(2,1)} async-done(((bf16[32,4,640]{2,0,1:T(8,128)(2,1)}), bf16[32,4,640]{2,0,1:T(8,128)(2,1)}) %all-reduce.14.cloned.1.call-update) | async-done | bytes 163856
  541.0 62.7 %psum.45 = f32[32,4]{0,1:T(4,128)S(1)} all-reduce(f32[32,4]{0,1:T(4,128)S(1)} %multiply_reduce_fusion), channel_id=1, replica_groups=mesh['grp'=8,'seq'=16] {'grp','seq'}, use_global_device_ids=true, to_apply=%region_33.35 | all-reduce | flops 128 | bytes 1024 | tf_op jit(solution)/shard_map/psum | solution.py:202
  604.8 23.7 %all_gather.11 = bf16[32,4,640]{0,1,2:T(4,128)(2,1)S(1)} all-gather(bf16[32,4,40]{0,1,2:T(4,128)(2,1)S(1)} %copy.133), channel_id=1, replica_groups=mesh['grp'=8,'seq'=16] {'seq'}, dimensions={2}, use_global_device_ids=true | all-gather | bytes 174080 | tf_op jit(solution)/shard_map/all_gather | solution.py:206
  631.3 58.0 %all-reduce.18.cloned.1.call-done = (bf16[32,4,864]{2,0,1:T(8,128)(2,1)}, bf16[32,4,864]{2,0,1:T(8,128)(2,1)}) async-done(((bf16[32,4,864]{2,0,1:T(8,128)(2,1)}, bf16[32,4,864]{2,0,1:T(8,128)(2,1)}), (bf16[32,4,864]{2,0,1:T(8,128)(2,1)}, bf16[32,4,864]{2,0,1:T(8,128)(2,1)})) %all-reduce.18.cloned.1.call-update) | async-done | bytes 442384 | tf_op jit(solution)/shard_map/psum | solution.py:211
  691.9 84.0 %all-reduce.16.cloned.1.call-done = bf16[32,4,640]{2,0,1:T(8,128)(2,1)} async-done(((bf16[32,4,640]{2,0,1:T(8,128)(2,1)}), bf16[32,4,640]{2,0,1:T(8,128)(2,1)}) %all-reduce.16.cloned.1.call-update) | async-done | bytes 163856
  (239 shorter events, 87.9 us)
Async XLA Ops:
  6.5 622.4 %copy-start = (bf16[640,864]{0,1:T(8,128)(2,1)S(1)}, bf16[640,864]{0,1:T(8,128)(2,1)}, u32[]{:S(2)}) copy-start(bf16[640,864]{0,1:T(8,128)(2,1)} %param.36) | copy-start | bytes 3317764
  6.5 154.0 %all-reduce.12.cloned.1.call-start = ((), (), s32[]{:S(2)}) async-start(), calls=%async_computation.2 | async-start | bytes 262144
  8.0 70.5 %copy-start.19 = (pred[32]{0:T(512)(128)(4,1)}, pred[32]{0:T(512)(128)(4,1)S(1)}, u32[]{:S(2)}) copy-start(pred[32]{0:T(512)(128)(4,1)S(1)} %compare_and_fusion.5) | copy-start | bytes 100
  78.6 24.0 %copy-start.23 = (s32[32]{0:T(128)S(1)}, s32[32]{0:T(128)}, u32[]{:S(2)}) copy-start(s32[32]{0:T(128)} %param.26) | copy-start | bytes 388
  78.6 24.1 %copy-start.1 = (s32[32]{0:T(128)S(1)}, s32[32]{0:T(128)}, u32[]{:S(2)}) copy-start(s32[32]{0:T(128)} %param.25) | copy-start | bytes 388
  100.3 6.4 copy-start.16
  100.3 7.7 copy-start.26
  100.3 60.2 %copy-start.21 = (f32[448]{0:T(512)S(1)}, f32[448]{0:T(512)}, u32[]{:S(2)}) copy-start(f32[448]{0:T(512)} %param.32) | copy-start | bytes 5380
  162.3 17.1 %all-to-all-start = ((f32[16,4,4,448]{3,2,1,0:T(4,128)}), f32[16,4,4,448]{3,2,1,0:T(4,128)S(1)}, u32[]{:S(2)}, u32[]{:S(2)}) async-start(f32[16,4,4,448]{3,2,1,0:T(4,128)} %stack.64), calls=%async_computation | async-start | bytes 1048576 | tf_op jit(solution)/shard_map/all_to_all | solution.py:100
  169.2 273.0 %all-reduce.10.cloned.1.call-start = ((), (), s32[]{:S(2)}) async-start(), calls=%async_computation.1 | async-start | bytes 327680 | tf_op jit(solution)/shard_map/psum | solution.py:182
  169.3 54.4 %copy-start.13 = (pred[20,4]{0,1:T(4,128)(4,1)}, pred[20,4]{0,1:T(4,128)(4,1)S(1)}, u32[]{:S(2)}) copy-start(pred[20,4]{0,1:T(4,128)(4,1)S(1)} %fusion.115) | copy-start | bytes 244
  180.1 4.3 copy-start.8
  182.2 1.5 copy-start.17
  182.2 2.4 copy-start.9
  210.0 4.1 copy-start.14
  334.4 122.2 %copy-start.7 = (bf16[320,640]{1,0:T(8,128)(2,1)S(1)}, bf16[320,640]{1,0:T(8,128)(2,1)}, u32[]{:S(2)}) copy-start(bf16[320,640]{1,0:T(8,128)(2,1)} %param.33) | copy-start | bytes 1228804
  336.3 203.8 %all-reduce.14.cloned.1.call-start = ((), (), s32[]{:S(2)}) async-start(), calls=%async_computation.3 | async-start | bytes 327680
  372.5 85.1 %copy-start.25 = (u32[128]{0:T(128)S(1)}, u32[128]{0:T(128)}, u32[]{:S(2)}) copy-start(u32[128]{0:T(128)} %constant.254) | copy-start | bytes 1540
  372.5 85.7 %copy-start.24 = (s32[32]{0:T(128)S(1)}, s32[32]{0:T(128)}, u32[]{:S(2)}) copy-start(s32[32]{0:T(128)} %param.26) | copy-start | bytes 388
  372.5 167.5 %copy-start.20 = (pred[32]{0:T(512)(128)(4,1)S(1)}, pred[32]{0:T(512)(128)(4,1)}, u32[]{:S(2)}) copy-start(pred[32]{0:T(512)(128)(4,1)} %copy-done.19) | copy-start | bytes 100
  372.5 231.2 %copy-start.22 = (f32[40]{0:T(128)S(1)}, f32[40]{0:T(128)}, u32[]{:S(2)}) copy-start(f32[40]{0:T(128)} %param.34) | copy-start | bytes 484
  457.6 231.7 %all-reduce.18.cloned.1.call-start = ((), (), s32[]{:S(2)}) async-start(), calls=%async_computation.5 | async-start | bytes 917504 | tf_op jit(solution)/shard_map/psum | solution.py:211
  628.5 1.5 copy-start.6
  631.2 144.6 %all-reduce.16.cloned.1.call-start = ((), (), s32[]{:S(2)}) async-start(), calls=%async_computation.4 | async-start | bytes 327680
  (12 other events, 12.3 us)
Sparse Core Ops, SparseCore 0:
  102.7 57.7 all-reduce.11
  336.4 105.8 all-reduce.9
  457.7 82.3 all-reduce.13
  631.3 57.8 all-reduce.17
  692.4 83.4 all-reduce.15
